TPU v7x, 32 devices: a whole 2x2x4 slice. The times are simulated.
32 devices in a mesh: rep: 2 (over x), shard: 16 (over z, y, core).
Axes of the slice: x: 2, y: 2, z: 4, core: 2. Of those that a mesh axis runs over, the one named last changes fastest.
Arguments:
- tokens: bfloat16 [2, 32, 64, 1024], P(None, ('rep', 'shard')), may hold values from -6 to 6
- prefix: int32 [2, 32], P(None, ('rep', 'shard')), may hold values from 6 to 32
- qkv_weight: bfloat16 [1024, 3072], P('shard'), may hold values from -0.1875 to 0.1875
- out_weight: bfloat16 [1024, 1024], P('shard'), may hold values from -1 to 1
- in_weight: bfloat16 [1024, 5632], P('shard'), may hold values from -0.1875 to 0.1875
- down_weight: bfloat16 [2816, 1024], P('shard'), may hold values from -0.109375 to 0.109375
- cotangent: bfloat16 [2, 32, 64, 1024], P(None, ('rep', 'shard')), may hold values from -6 to 6
Outputs:
- result: bfloat16 [2, 32, 64, 1024], P(None, ('rep', 'shard'))
- grad_tokens: float32 [2, 32, 64, 1024], P(None, ('rep', 'shard'))
- grad_qkv: float32 [1024, 3072], P('shard')
- grad_out: float32 [1024, 1024], P('shard')
- grad_in: float32 [1024, 5632], P('shard')
- grad_down: float32 [2816, 1024], P('shard')
Inputs may be any that keep to these rules, and one draw needn't show every extreme that they name: Each sequence's prefix length, a tenth to a half of 64.
All inputs are finite; a program needn't handle non-finite values.
Results may differ from a plain program's by a relative error of at most 0.014.
Values may be sent and summed in bfloat16 or wider, within the bound.
No kernel may reach another device: no remote copies, remote signals or barrier semaphores. Data moves between devices by JAX's collectives and lax.ppermute only.
A program may use at most 256 MiB of HBM per device.

v0:
```python
import jax
import jax.numpy as jnp
from jax import lax
from jax.sharding import PartitionSpec as P

H = 16
HD = 64


def norm_rows(values):
    centre = values - jnp.mean(values, axis=-1, keepdims=True)
    inverse = lax.rsqrt(jnp.mean(centre * centre, axis=-1, keepdims=True) + 1e-05)
    return (centre * inverse, inverse)


def norm_back(normed, inverse, upstream):
    return inverse * (
        upstream
        - jnp.mean(upstream, axis=-1, keepdims=True)
        - normed * jnp.mean(upstream * normed, axis=-1, keepdims=True)
    )


def rope_tables(length, head_size):
    position = jnp.arange(length, dtype=jnp.float32)[:, None]
    frequency = 10000.0 ** (-jnp.arange(0, head_size, 2, dtype=jnp.float32) / head_size)
    angles = position * frequency[None, :]
    angles = jnp.concatenate([angles, angles], axis=-1)
    return (jnp.cos(angles)[:, None, :], jnp.sin(angles)[:, None, :])


def rotate(values, cosine, sine):
    half_size = values.shape[-1] // 2
    turned = jnp.concatenate([-values[..., half_size:], values[..., :half_size]], axis=-1)
    return values * cosine + turned * sine


def rotate_back(grads, cosine, sine):
    half_size = grads.shape[-1] // 2
    scaled = grads * sine
    return grads * cosine + jnp.concatenate(
        [scaled[..., half_size:], -scaled[..., :half_size]], axis=-1
    )


def transpose_dot(left, right):
    return lax.dot_general(
        left, right, (((1,), (1,)), ((), ())), preferred_element_type=jnp.float32
    )


def inner_rows(left, right):
    return lax.dot_general(
        left, right, (((0,), (0,)), ((), ())), preferred_element_type=jnp.float32
    )


def masked_scores(query, keys, allowed, scale):
    scores = jnp.einsum("lhe,mhe->hlm", query, keys, preferred_element_type=jnp.float32) * scale
    return jnp.where(allowed[None], scores, -1e30)


def attend(query, keys, values, allowed, scale):
    scores = masked_scores(query, keys, allowed, scale)
    highest = jnp.max(scores, axis=-1, keepdims=True)
    expo = jnp.exp(scores - highest)
    summed = jnp.sum(expo, axis=-1, keepdims=True)
    probs = (expo / summed).astype(jnp.bfloat16)
    output = jnp.einsum("hlm,mhe->lhe", probs, values, preferred_element_type=jnp.float32)
    return (output, highest + jnp.log(summed))


def attend_back(query, keys, values, log_total, grad_out, allowed, scale):
    probs = jnp.exp(masked_scores(query, keys, allowed, scale) - log_total)
    dprob = jnp.einsum("lhe,mhe->hlm", grad_out, values, preferred_element_type=jnp.float32)
    centre = jnp.sum(probs * dprob, axis=-1, keepdims=True)
    dscore = (probs * (dprob - centre)).astype(jnp.bfloat16)
    dquery = jnp.einsum("hlm,mhe->lhe", dscore, keys, preferred_element_type=jnp.float32) * scale
    dkeys = jnp.einsum("hlm,lhe->mhe", dscore, query, preferred_element_type=jnp.float32) * scale
    dvalues = jnp.einsum(
        "hlm,lhe->mhe", probs.astype(jnp.bfloat16), grad_out, preferred_element_type=jnp.float32
    )
    return (dquery, dkeys, dvalues)


def local(tokens, prefix, qkv_weight, out_weight, in_weight, down_weight, cotangent):
    micro = tokens.shape[0]
    length = tokens.shape[2]
    width = tokens.shape[3]
    hidden_units = down_weight.shape[0] * lax.axis_size("shard")
    scale = HD ** (-0.5)
    cosine, sine = rope_tables(length, HD)
    row_pos = lax.broadcasted_iota(jnp.int32, (length, length), 0)
    col_pos = lax.broadcasted_iota(jnp.int32, (length, length), 1)
    full_set = (
        lax.all_gather(qkv_weight, "shard", axis=0, tiled=True),
        lax.all_gather(out_weight, "shard", axis=0, tiled=True),
        lax.all_gather(in_weight, "shard", axis=0, tiled=True),
        lax.all_gather(down_weight, "shard", axis=0, tiled=True),
    )
    outputs = []
    grad_inputs = []
    kept_h1, kept_gqkv, kept_attn, kept_ga, kept_h2, kept_ggu, kept_hid, kept_gm = (
        [],
        [],
        [],
        [],
        [],
        [],
        [],
        [],
    )
    for batch_index in range(micro):
        xrow = tokens[batch_index, 0].astype(jnp.float32)
        normed_one, inverse_one = norm_rows(xrow)
        first_in = normed_one.astype(jnp.bfloat16)
        mixed = jnp.dot(first_in, full_set[0], preferred_element_type=jnp.float32)
        query = rotate(mixed[:, :width].reshape(length, H, HD), cosine, sine).astype(jnp.bfloat16)
        keys = rotate(mixed[:, width : 2 * width].reshape(length, H, HD), cosine, sine).astype(
            jnp.bfloat16
        )
        values = mixed[:, 2 * width :].reshape(length, H, HD).astype(jnp.bfloat16)
        allowed = (col_pos <= row_pos) | (col_pos < prefix[batch_index, 0])
        attended, log_total = attend(query, keys, values, allowed, scale)
        attn_low = attended.reshape(length, width).astype(jnp.bfloat16)
        middle = xrow + jnp.dot(attn_low, full_set[1], preferred_element_type=jnp.float32)
        normed_two, inverse_two = norm_rows(middle)
        second_in = normed_two.astype(jnp.bfloat16)
        gate_up = jnp.dot(second_in, full_set[2], preferred_element_type=jnp.float32)
        up_part = gate_up[:, :hidden_units]
        gate_part = gate_up[:, hidden_units:]
        sigmoid = jax.nn.sigmoid(gate_part)
        hidden = (gate_part * sigmoid * up_part).astype(jnp.bfloat16)
        final = middle + jnp.dot(hidden, full_set[3], preferred_element_type=jnp.float32)
        outputs.append(final.astype(jnp.bfloat16))
        grad_final = cotangent[batch_index, 0].astype(jnp.float32)
        grad_m = grad_final.astype(jnp.bfloat16)
        grad_hidden = transpose_dot(grad_m, full_set[3])
        grad_up = grad_hidden * (gate_part * sigmoid)
        grad_gate = grad_hidden * up_part * (sigmoid * (1.0 + gate_part * (1.0 - sigmoid)))
        grad_gu = jnp.concatenate([grad_up, grad_gate], axis=-1).astype(jnp.bfloat16)
        grad_mid = grad_final + norm_back(
            normed_two, inverse_two, transpose_dot(grad_gu, full_set[2])
        )
        grad_branch = grad_mid.astype(jnp.bfloat16)
        grad_att = transpose_dot(grad_branch, full_set[1]).astype(jnp.bfloat16)
        dquery, dkeys, dvalues = attend_back(
            query, keys, values, log_total, grad_att.reshape(length, H, HD), allowed, scale
        )
        dquery = rotate_back(dquery, cosine, sine).reshape(length, width)
        dkeys = rotate_back(dkeys, cosine, sine).reshape(length, width)
        grad_mixed = jnp.concatenate(
            [dquery, dkeys, dvalues.reshape(length, width)], axis=-1
        ).astype(jnp.bfloat16)
        grad_input = grad_mid + norm_back(
            normed_one, inverse_one, transpose_dot(grad_mixed, full_set[0])
        )
        grad_inputs.append(grad_input)
        kept_h1.append(first_in)
        kept_gqkv.append(grad_mixed)
        kept_attn.append(attn_low)
        kept_ga.append(grad_branch)
        kept_h2.append(second_in)
        kept_ggu.append(grad_gu)
        kept_hid.append(hidden)
        kept_gm.append(grad_m)
    all_h1 = jnp.concatenate(kept_h1, axis=0)
    all_gqkv = jnp.concatenate(kept_gqkv, axis=0)
    all_attn = jnp.concatenate(kept_attn, axis=0)
    all_ga = jnp.concatenate(kept_ga, axis=0)
    all_h2 = jnp.concatenate(kept_h2, axis=0)
    all_ggu = jnp.concatenate(kept_ggu, axis=0)
    all_hid = jnp.concatenate(kept_hid, axis=0)
    all_gm = jnp.concatenate(kept_gm, axis=0)
    part_one = inner_rows(all_h1, all_gqkv)
    part_two = inner_rows(all_attn, all_ga)
    part_three = inner_rows(all_h2, all_ggu)
    row_share = lax.psum_scatter(
        jnp.concatenate([part_one, part_two, part_three], axis=1),
        "shard",
        scatter_dimension=0,
        tiled=True,
    )
    down_share = lax.psum_scatter(
        inner_rows(all_hid, all_gm), "shard", scatter_dimension=0, tiled=True
    )
    grad_qkv, grad_out, grad_in, grad_down = (
        lax.psum(row_share[:, : 3 * width].astype(jnp.bfloat16), "rep").astype(jnp.float32),
        lax.psum(row_share[:, 3 * width : 4 * width].astype(jnp.bfloat16), "rep").astype(
            jnp.float32
        ),
        lax.psum(row_share[:, 4 * width :].astype(jnp.bfloat16), "rep").astype(jnp.float32),
        lax.psum(down_share.astype(jnp.bfloat16), "rep").astype(jnp.float32),
    )
    result = jnp.stack(outputs, axis=0)[:, None]
    grad_tokens = jnp.stack(grad_inputs, axis=0)[:, None]
    return (result, grad_tokens, grad_qkv, grad_out, grad_in, grad_down)


def solution(mesh):
    placed = (
        P(None, ("rep", "shard"), None, None),
        P(None, ("rep", "shard")),
        P("shard", None),
        P("shard", None),
        P("shard", None),
        P("shard", None),
        P(None, ("rep", "shard"), None, None),
    )
    return jax.shard_map(
        local,
        mesh=mesh,
        in_specs=placed,
        out_specs=(
            P(None, ("rep", "shard"), None, None),
            P(None, ("rep", "shard"), None, None),
            P("shard", None),
            P("shard", None),
            P("shard", None),
            P("shard", None),
        ),
        check_vma=False,
    )
```

profile of v0, /device:TPU:0, one launch (start us, length us, event | category | flops | bytes accessed | tf_op | source)
XLA Modules:
  0.0 870.6 jit_solution(7404513328902034223)
XLA Ops:
  10.0 1.3 fusion.149
  13.4 1.1 convert_reduce_fusion.1
  14.6 1.2 fusion.91
  16.0 1.7 slice_bitcast_fusion.1
  17.9 57.0 %all-gather.5.cloned.1.call-done = bf16[1024,3072]{1,0:T(8,128)(2,1)} async-done(((bf16[64,3072]{1,0:T(8,128)(2,1)}), bf16[1024,3072]{1,0:T(8,128)(2,1)}) %all-gather.5.cloned.1.call-update) | async-done | bytes 6291472 | tf_op jit(solution)/shard_map/all_gather | solution.py:96
  74.9 4.0 fusion.154
  79.6 4.0 fusion.156
  83.6 0.9 convert_element_type.150
  85.2 1.3 fusion.55
  87.9 29.1 %all-gather.7.cloned.1.call-done = bf16[1024,1024]{1,0:T(8,128)(2,1)} async-done(((bf16[64,1024]{1,0:T(8,128)(2,1)}), bf16[1024,1024]{1,0:T(8,128)(2,1)}) %all-gather.7.cloned.1.call-update) | async-done | bytes 2097168 | tf_op jit(solution)/shard_map/all_gather | solution.py:97
  117.0 2.3 fusion.153
  119.6 1.3 fusion.150
  123.6 88.8 %all-gather.9.cloned.1.call-done = bf16[1024,5632]{1,0:T(8,128)(2,1)} async-done(((bf16[64,5632]{1,0:T(8,128)(2,1)}), bf16[1024,5632]{1,0:T(8,128)(2,1)}) %all-gather.9.cloned.1.call-update) | async-done | bytes 11534352 | tf_op jit(solution)/shard_map/all_gather | solution.py:98
  212.4 7.7 fusion.157
  220.2 3.3 fusion.155
  223.5 48.3 %all-gather.11.cloned.1.call-done = bf16[2816,1024]{1,0:T(8,128)(2,1)} async-done(((bf16[176,1024]{1,0:T(8,128)(2,1)}), bf16[2816,1024]{1,0:T(8,128)(2,1)}) %all-gather.11.cloned.1.call-update) | async-done | bytes 5767184 | tf_op jit(solution)/shard_map/all_gather | solution.py:99
  271.8 5.9 multiply_convert_fusion.1
  277.8 2.8 multiply_convert_fusion.3
  280.6 0.8 copy-done.20
  281.3 6.1 fusion.46
  289.0 8.9 %fusion.140 = (f32[64]{0:T(128)S(1)}, f32[64]{0:T(128)S(1)}, f32[64,1024]{1,0:T(8,128)S(1)}) fusion(f32[64]{0:T(128)} %copy-done.65, f32[64,1024]{1,0:T(8,128)} %copy-done.3, f32[64]{0:T(128)} %copy-done.57, bf16[1024,5632]{1,0:T(8,128)(2,1)} %all-gather.9.cloned.1.call-done, bf16[64,2816]{1,0:T(8,128)(2,1)} %get-tuple-element.35, ...), kind=kOutput, calls=%fused_computation.237 | convolution fusion | flops 739966848 | bytes 12780544 | tf_op jit(solution)/shard_map/dot_general | solution.py:47
  298.0 9.5 %fusion.139 = (f32[64]{0:T(128)S(1)}, f32[64]{0:T(128)S(1)}, f32[64,1024]{1,0:T(8,128)S(1)}) fusion(f32[64]{0:T(128)S(1)} %copy-done.64, f32[64,1024]{1,0:T(8,128)S(1)} %get-tuple-element.91, f32[64]{0:T(128)S(1)} %copy-done.56, bf16[1024,5632]{1,0:T(8,128)(2,1)} %all-gather.9.cloned.1.call-done, bf16[64,2816]{1,0:T(8,128)(2,1)S(1)} %copy-done.26, ...), kind=kOutput, calls=%fused_computation.236 | convolution fusion | flops 739966848 | bytes 12780544 | tf_op jit(solution)/shard_map/dot_general | solution.py:47
  307.6 1.1 fusion.141
  309.3 1.4 convolution_convert_fusion.4
  310.7 1.8 copy.66
  312.5 2.3 convolution_convert_fusion.5
  314.8 1.1 copy.65
  316.0 1.9 fusion.97
  321.8 6.5 fusion.26
  328.3 10.9 %fusion = f32[1024,5632]{1,0:T(8,128)} fusion(bf16[64,2816]{1,0:T(8,128)(2,1)S(1)} %copy-done.23, bf16[64,2816]{1,0:T(8,128)(2,1)S(1)} %copy-done.22, bf16[64,2816]{1,0:T(8,128)(2,1)S(1)} %copy-done.27, bf16[64,2816]{1,0:T(8,128)(2,1)S(1)} %copy-done.25, bf16[64,1024]{1,0:T(8,128)(2,1)S(1)} %copy-done.16, bf16[64,1024]{1,0:T(8,128)(2,1)S(1)} %fusion.122), kind=kOutput, calls=%fused_computation.1 | convolution fusion | flops 1482686464 | bytes 24772608 | tf_op jit(solution)/shard_map/dot_general | solution.py:53
  339.2 26.3 %pad_maximum_fusion = f32[1024,9728]{1,0:T(8,128)} fusion(f32[1024,5632]{1,0:T(8,128)} %fusion, f32[1024,1024]{1,0:T(8,128)S(1)} %fusion.97, f32[1024,3072]{1,0:T(8,128)} %fusion.26), kind=kLoop, calls=%fused_computation | loop fusion | flops 19922944 | bytes 79691776 | tf_op jit(solution)/shard_map/concatenate | solution.py:179
  365.6 0.9 copy-done.5
  366.6 3.9 fusion.12
  370.5 3.9 fusion.13
  375.1 4.8 fusion.20
  380.0 32.5 %reduce-scatter.5.cloned.1.call-done = f32[176,1024]{1,0:T(8,128)} async-done(((f32[2816,1024]{1,0:T(8,128)}), f32[176,1024]{1,0:T(8,128)}) %reduce-scatter.5.cloned.1.call-update) | async-done | bytes 720912 | tf_op jit(solution)/shard_map/reduce_scatter | solution.py:184
  412.5 1.9 convert_element_type.173
  414.4 386.4 %reduce-scatter.3.cloned.1.call-done = f32[64,9728]{1,0:T(8,128)} async-done(((f32[1024,9728]{1,0:T(8,128)}), f32[64,9728]{1,0:T(8,128)}) %reduce-scatter.3.cloned.1.call-update) | async-done | bytes 2490384 | tf_op jit(solution)/shard_map/reduce_scatter | solution.py:178
  800.7 1.8 convert.61
  803.3 0.8 slice.171
  804.1 0.9 slice.173
  805.1 5.0 fusion.138
  810.4 0.8 maximum_bitcast_fusion
  811.2 45.8 %all-reduce.3.cloned.1.call-done = (bf16[64,3072]{1,0:T(8,128)(2,1)}, bf16[64,1024]{1,0:T(8,128)(2,1)}, bf16[64,5632]{1,0:T(8,128)(2,1)}, bf16[176,1024]{1,0:T(8,128)(2,1)}) async-done(((bf16[64,3072]{1,0:T(8,128)(2,1)}, bf16[64,1024]{1,0:T(8,128)(2,1)}, bf16[64,5632]{1,0:T(8,128)(2,1)}, bf16[176,1024]{1,0:T(8,128)(2,1)}), (bf16[64,3072]{1,0:T(8,128)(2,1)}, bf16[64,1024]{1,0:T(8,128)(2,1)}, ...) | async-done | bytes 1605648 | tf_op jit(solution)/shard_map/psum | solution.py:188
  857.0 1.7 convert_element_type.171
  858.7 1.9 convert_element_type.170
  860.7 1.9 convert_element_type.174
  862.6 1.2 convert_element_type.172
  (212 shorter events, 18.6 us)
Async XLA Ops:
  7.2 10.5 %copy-start.6 = (bf16[2,1,64,1024]{3,2,1,0:T(8,128)(2,1)S(1)}, bf16[2,1,64,1024]{3,2,1,0:T(8,128)(2,1)}, u32[]{:S(2)}) copy-start(bf16[2,1,64,1024]{3,2,1,0:T(8,128)(2,1)} %param.7) | copy-start | bytes 786436
  7.2 67.7 %all-gather.5.cloned.1.call-start = ((), (), s32[]{:S(2)}) async-start(), calls=%async_computation.2 | async-start | bytes 6684672 | tf_op jit(solution)/shard_map/all_gather | solution.py:96
  7.9 109.1 %all-gather.7.cloned.1.call-start = ((), (), s32[]{:S(2)}) async-start(), calls=%async_computation.3 | async-start | bytes 2228224 | tf_op jit(solution)/shard_map/all_gather | solution.py:97
  8.7 203.8 %all-gather.9.cloned.1.call-start = ((), (), s32[]{:S(2)}) async-start(), calls=%async_computation.4 | async-start | bytes 12255232 | tf_op jit(solution)/shard_map/all_gather | solution.py:98
  9.4 262.4 %all-gather.11.cloned.1.call-start = ((), (), s32[]{:S(2)}) async-start(), calls=%async_computation.5 | async-start | bytes 6127616 | tf_op jit(solution)/shard_map/all_gather | solution.py:99
  10.0 402.5 %reduce-scatter.5.cloned.1.call-start = ((), (), s32[]{:S(2)}) async-start(), calls=%async_computation.7 | async-start | bytes 12255232 | tf_op jit(solution)/shard_map/reduce_scatter | solution.py:184
  14.6 60.3 %copy-start.51 = (f32[64]{0:T(128)}, f32[64]{0:T(128)S(1)}, u32[]{:S(2)}) copy-start(f32[64]{0:T(128)S(1)} %get-tuple-element.100) | copy-start | bytes 772
  14.6 60.3 %copy-start.53 = (f32[64]{0:T(128)}, f32[64]{0:T(128)S(1)}, u32[]{:S(2)}) copy-start(f32[64]{0:T(128)S(1)} %get-tuple-element.101) | copy-start | bytes 772
  15.8 59.1 %copy-start.59 = (f32[64]{0:T(128)}, f32[64]{0:T(128)S(1)}, u32[]{:S(2)}) copy-start(f32[64]{0:T(128)S(1)} %add_rsqrt_fusion.3) | copy-start | bytes 772
  15.8 59.1 %copy-start.61 = (f32[64]{0:T(128)}, f32[64]{0:T(128)S(1)}, u32[]{:S(2)}) copy-start(f32[64]{0:T(128)S(1)} %add_rsqrt_fusion.1) | copy-start | bytes 772
  17.9 61.0 %copy-start.28 = (bf16[64,1024]{1,0:T(8,128)(2,1)}, bf16[64,1024]{1,0:T(8,128)(2,1)S(1)}, u32[]{:S(2)}) copy-start(bf16[64,1024]{1,0:T(8,128)(2,1)S(1)} %get-tuple-element.64) | copy-start | bytes 393220
  17.9 61.7 %copy-start.30 = (bf16[64,1024]{1,0:T(8,128)(2,1)}, bf16[64,1024]{1,0:T(8,128)(2,1)S(1)}, u32[]{:S(2)}) copy-start(bf16[64,1024]{1,0:T(8,128)(2,1)S(1)} %get-tuple-element.65) | copy-start | bytes 393220
  79.1 8.5 copy-start.35
  87.6 32.0 %copy-start.49 = (f32[16,64]{1,0:T(8,128)}, f32[16,64]{1,0:T(8,128)S(1)}, u32[]{:S(2)}) copy-start(f32[16,64]{1,0:T(8,128)S(1)} %fusion.64) | copy-start | bytes 12292
  87.9 31.7 %copy-start.33 = (bf16[16,64,64]{2,1,0:T(8,128)(2,1)}, bf16[16,64,64]{2,1,0:T(8,128)(2,1)S(1)}, u32[]{:S(2)}) copy-start(bf16[16,64,64]{2,1,0:T(8,128)(2,1)S(1)} %convolution_convert_fusion.3) | copy-start | bytes 393220
  117.0 4.0 copy-start.37
  117.0 4.4 copy-start.1
  117.0 4.4 copy-start.7
  119.4 2.9 copy-start.55
  212.4 7.8 copy-start
  271.8 5.9 copy-start.2
  271.8 5.9 copy-start.17
  271.8 5.9 copy-start.41
  277.8 2.8 copy-start.18
  277.8 3.6 copy-start.44
  277.8 3.6 copy-start.45
  287.5 513.3 %reduce-scatter.3.cloned.1.call-start = ((), (), s32[]{:S(2)}) async-start(), calls=%async_computation.6 | async-start | bytes 42336256 | tf_op jit(solution)/shard_map/reduce_scatter | solution.py:178
  289.0 9.0 %copy-start.24 = (bf16[64,2816]{1,0:T(8,128)(2,1)S(1)}, bf16[64,2816]{1,0:T(8,128)(2,1)}, u32[]{:S(2)}) copy-start(bf16[64,2816]{1,0:T(8,128)(2,1)} %get-tuple-element.32) | copy-start | bytes 1081348
  289.0 9.0 %copy-start.26 = (bf16[64,2816]{1,0:T(8,128)(2,1)S(1)}, bf16[64,2816]{1,0:T(8,128)(2,1)}, u32[]{:S(2)}) copy-start(bf16[64,2816]{1,0:T(8,128)(2,1)} %get-tuple-element.33) | copy-start | bytes 1081348
  289.0 9.0 %copy-start.56 = (f32[64]{0:T(128)S(1)}, f32[64]{0:T(128)}, u32[]{:S(2)}) copy-start(f32[64]{0:T(128)} %copy-done.55) | copy-start | bytes 772
  289.0 9.0 %copy-start.64 = (f32[64]{0:T(128)S(1)}, f32[64]{0:T(128)}, u32[]{:S(2)}) copy-start(f32[64]{0:T(128)} %copy-done.63) | copy-start | bytes 772
  298.0 9.6 %copy-start.4 = (f32[64,1024]{1,0:T(8,128)S(1)}, f32[64,1024]{1,0:T(8,128)}, u32[]{:S(2)}) copy-start(f32[64,1024]{1,0:T(8,128)} %copy-done.3) | copy-start | bytes 786436
  298.0 9.6 %copy-start.42 = (bf16[2,1,64,1024]{3,2,1,0:T(8,128)(2,1)S(1)}, bf16[2,1,64,1024]{3,2,1,0:T(8,128)(2,1)}, u32[]{:S(2)}) copy-start(bf16[2,1,64,1024]{3,2,1,0:T(8,128)(2,1)} %param.13) | copy-start | bytes 786436
  298.0 9.6 %copy-start.58 = (f32[64]{0:T(128)S(1)}, f32[64]{0:T(128)}, u32[]{:S(2)}) copy-start(f32[64]{0:T(128)} %copy-done.57) | copy-start | bytes 772
  298.0 9.6 %copy-start.66 = (f32[64]{0:T(128)S(1)}, f32[64]{0:T(128)}, u32[]{:S(2)}) copy-start(f32[64]{0:T(128)} %copy-done.65) | copy-start | bytes 772
  314.8 3.1 copy-start.9
  314.8 3.1 copy-start.38
  321.8 6.5 copy-start.16
  321.8 6.5 copy-start.22
  321.8 6.5 copy-start.23
  321.8 6.5 copy-start.25
  321.8 6.5 copy-start.27
  365.5 5.0 copy-start.21
  365.6 491.5 %all-reduce.3.cloned.1.call-start = ((), (), s32[]{:S(2)}) async-start(), calls=%async_computation.8 | async-start | bytes 3211264 | tf_op jit(solution)/shard_map/psum | solution.py:188
  802.6 2.4 copy-start.8
  805.0 5.1 copy-start.39
  805.0 5.1 copy-start.40
  857.0 5.5 copy-start.43
  (26 other events, 31.8 us)
Sparse Core Ops, SparseCore 0:
  10.3 64.5 all-gather.4
  77.0 39.9 all-gather.6
  119.3 93.0 all-gather.8
  214.6 57.1 all-gather.10
  287.6 124.8 reduce-scatter.4
  417.3 383.4 reduce-scatter.2
  805.1 51.8 all-reduce.2
where the time goes:
time: 871 us
  waiting for transfers between devices  690 us (79%)
  matrix products  100 us (11%)
  other arithmetic  49.7 us (6%)
  between operations  15.2 us (2%)
  local copies, waits for them, and re-layouts  14.9 us (2%)
    reduce_scatter x1, waiting for transfers between devices, local(): lax.psum_scatter(jnp.concatenate([part_one, part_two, part_three], axis=1...  386 us
    all_gather x1, waiting for transfers between devices, local(): lax.all_gather(in_weight, 'shard', axis=0, tiled=True)  88.8 us
    all_gather x1, waiting for transfers between devices, local(): lax.all_gather(qkv_weight, 'shard', axis=0, tiled=True)  57 us
    all_gather x1, waiting for transfers between devices, local(): lax.all_gather(down_weight, 'shard', axis=0, tiled=True)  48.3 us
    psum x1, waiting for transfers between devices, local(): lax.psum(row_share[:, :3 * width].astype(jnp.bfloat16), 'rep')  45.8 us
    dot_general x8, matrix products, transpose_dot(): lax.dot_general(left, right, (((1,), (1,)), ((), ())), preferred_element_...  40.7 us
    reduce_scatter x1, waiting for transfers between devices, local(): lax.psum_scatter(inner_rows(all_hid, all_gm), 'shard', scatter_dimension=...  32.5 us
    all_gather x1, waiting for transfers between devices, local(): lax.all_gather(out_weight, 'shard', axis=0, tiled=True)  29.1 us
  transfers between devices with their start and end apart: 7, of which 7 were waited for; matrix products, arithmetic and copies ran while one was open for 15% of the time, Pallas kernels for 0%

commit v1 on v0

--- a/solution.py
+++ b/solution.py
@@ -5,6 +5,18 @@
 
 H = 16
 HD = 64
+
+
+def doubled_up(x, axis, dim):
+    ways, here = (lax.axis_size(axis), lax.axis_index(axis))
+    grown, reach = (x, 1)
+    while reach < ways:
+        theirs = lax.ppermute(grown, axis, [(d, d ^ reach) for d in range(ways)])
+        mine_first = jnp.concatenate([grown, theirs], axis=dim)
+        theirs_first = jnp.concatenate([theirs, grown], axis=dim)
+        grown = jnp.where(here & reach == 0, mine_first, theirs_first)
+        reach = 2 * reach
+    return grown
 
 
 def norm_rows(values):
@@ -95,7 +107,7 @@
     full_set = (
         lax.all_gather(qkv_weight, "shard", axis=0, tiled=True),
         lax.all_gather(out_weight, "shard", axis=0, tiled=True),
-        lax.all_gather(in_weight, "shard", axis=0, tiled=True),
+        doubled_up(in_weight, "shard", 0),
         lax.all_gather(down_weight, "shard", axis=0, tiled=True),
     )
     outputs = []

time: 871 us -> 1090 us (1.25)
  waiting for transfers between devices: 690 us -> 877 us
  other arithmetic: 49.7 us -> 72.5 us
    ppermute x0 -> x4, waiting for transfers between devices: none -> 407 us  [doubled_up(): theirs = lax.ppermute(grown, axis, [(d, d ^ reach) for d in range(ways)])]
    all_gather x1 -> x0, waiting for transfers between devices: 88.8 us -> none  [local(): lax.all_gather(in_weight, 'shard', axis=0, tiled=True)]
    all_gather x1, waiting for transfers between devices: 57 us -> 0.02 us  [local(): lax.all_gather(qkv_weight, 'shard', axis=0, tiled=True)]
    all_gather x1, waiting for transfers between devices: 48.3 us -> 0.01 us  [local(): lax.all_gather(down_weight, 'shard', axis=0, tiled=True)]
    all_gather x1, waiting for transfers between devices: 29.1 us -> 0.01 us  [local(): lax.all_gather(out_weight, 'shard', axis=0, tiled=True)]
    select_n x0 -> x4, other arithmetic: none -> 28.3 us  [doubled_up(): grown = jnp.where(here & reach == 0, mine_first, theirs_first)]
  transfers between devices with their start and end apart: 7 -> 10, of which waited for: 7 -> 7; matrix products, arithmetic and copies ran while one was open for 15% -> 14% of each run, Pallas kernels for 0% -> 0%
where the time goes in v1:
time: 1090 us
  waiting for transfers between devices  877 us (80%)
  matrix products  101 us (9%)
  other arithmetic  72.5 us (7%)
  between operations  15.6 us (1%)
  local copies, waits for them, and re-layouts  13.1 us (1%)
    ppermute x4, waiting for transfers between devices, doubled_up(): theirs = lax.ppermute(grown, axis, [(d, d ^ reach) for d in range(ways)])  407 us
    reduce_scatter x1, waiting for transfers between devices, local(): lax.psum_scatter(jnp.concatenate([part_one, part_two, part_three], axis=1...  386 us
    psum x1, waiting for transfers between devices, local(): lax.psum(row_share[:, :3 * width].astype(jnp.bfloat16), 'rep')  45.8 us
    dot_general x8, matrix products, transpose_dot(): lax.dot_general(left, right, (((1,), (1,)), ((), ())), preferred_element_...  40.3 us
    reduce_scatter x1, waiting for transfers between devices, local(): lax.psum_scatter(inner_rows(all_hid, all_gm), 'shard', scatter_dimension=...  38.6 us
    select_n x4, other arithmetic, doubled_up(): grown = jnp.where(here & reach == 0, mine_first, theirs_first)  28.3 us
    dot_general x4, matrix products, inner_rows(): lax.dot_general(left, right, (((0,), (0,)), ((), ())), preferred_element_...  26.4 us
    concatenate x1, other arithmetic, local(): jnp.concatenate([part_one, part_two, part_three], axis=1)  24.9 us
  transfers between devices with their start and end apart: 10, of which 7 were waited for; matrix products, arithmetic and copies ran while one was open for 14% of the time, Pallas kernels for 0%

profile of v1, /device:TPU:0, one launch (start us, length us, event | category | flops | bytes accessed | tf_op | source)
XLA Modules:
  0.0 1087.5 jit_solution(15782246057137677276)
XLA Ops:
  8.5 2.0 collective-permute-done
  10.5 1.8 maximum_select_fusion.3
  12.3 3.0 collective-permute-start.1
  15.2 41.3 %collective-permute-done.1 = bf16[128,5632]{1,0:T(8,128)(2,1)} collective-permute-done((bf16[128,5632]{1,0:T(8,128)(2,1)S(1)}, bf16[128,5632]{1,0:T(8,128)(2,1)}, u32[]{:S(2)}, u32[]{:S(2)}) %collective-permute-start.1) | collective-permute-done | bytes 1441824 | tf_op jit(solution)/shard_map/ppermute | solution.py:14
  56.5 3.0 maximum_select_fusion.2
  59.6 1.6 collective-permute-start.2
  61.3 86.4 %collective-permute-done.2 = bf16[256,5632]{1,0:T(8,128)(2,1)} collective-permute-done((bf16[256,5632]{1,0:T(8,128)(2,1)S(1)}, bf16[256,5632]{1,0:T(8,128)(2,1)}, u32[]{:S(2)}, u32[]{:S(2)}) %collective-permute-start.2) | collective-permute-done | bytes 2883616 | tf_op jit(solution)/shard_map/ppermute | solution.py:14
  147.7 6.9 maximum_select_fusion.1
  154.6 2.5 collective-permute-start.3
  161.4 276.8 %collective-permute-done.3 = bf16[512,5632]{1,0:T(8,128)(2,1)} collective-permute-done((bf16[512,5632]{1,0:T(8,128)(2,1)}, bf16[512,5632]{1,0:T(8,128)(2,1)}, u32[]{:S(2)}, u32[]{:S(2)}) %collective-permute-start.3) | collective-permute-done | bytes 5767200 | tf_op jit(solution)/shard_map/ppermute | solution.py:14
  438.2 16.6 %maximum_select_fusion = bf16[1024,5632]{1,0:T(8,128)(2,1)} fusion(bf16[512,5632]{1,0:T(8,128)(2,1)} %collective-permute-done.3, bf16[512,5632]{1,0:T(8,128)(2,1)} %maximum_select_fusion.1, pred[]{:T(512)S(6)} %eq.12), kind=kLoop, calls=%fused_computation.1 | loop fusion | flops 51904512 | bytes 23068672 | tf_op jit(solution)/shard_map/jit(_where)/select_n | solution.py:17
  454.9 4.0 fusion.154
  459.5 4.0 fusion.156
  463.6 0.9 convert_element_type.150
  465.1 1.3 fusion.55
  467.5 1.0 convolution_convert_fusion.3
  468.5 2.4 fusion.153
  471.2 1.3 fusion.150
  474.6 7.6 fusion.157
  482.2 3.3 fusion.155
  485.6 5.9 multiply_convert_fusion.1
  491.5 2.8 multiply_convert_fusion.3
  495.1 6.4 fusion.46
  501.6 8.3 fusion.140
  509.9 9.5 fusion.139
  519.5 1.1 fusion.141
  521.2 1.4 convolution_convert_fusion.4
  522.7 1.8 copy.66
  524.5 2.4 convolution_convert_fusion.5
  526.9 1.1 copy.65
  528.1 1.9 fusion.97
  533.9 7.1 fusion.26
  541.0 11.0 %fusion = f32[1024,5632]{1,0:T(8,128)} fusion(bf16[64,2816]{1,0:T(8,128)(2,1)S(1)} %copy-done.24, bf16[64,2816]{1,0:T(8,128)(2,1)S(1)} %copy-done.23, bf16[64,2816]{1,0:T(8,128)(2,1)S(1)} %copy-done.28, bf16[64,2816]{1,0:T(8,128)(2,1)S(1)} %copy-done.26, bf16[64,1024]{1,0:T(8,128)(2,1)S(1)} %copy-done.17, bf16[64,1024]{1,0:T(8,128)(2,1)S(1)} %fusion.122), kind=kOutput, calls=%fused_computation.5 | convolution fusion | flops 1482686464 | bytes 24772608 | tf_op jit(solution)/shard_map/dot_general | solution.py:65
  552.1 24.9 %pad_maximum_fusion = f32[1024,9728]{1,0:T(8,128)} fusion(f32[1024,5632]{1,0:T(8,128)} %fusion, f32[1024,1024]{1,0:T(8,128)S(1)} %fusion.97, f32[1024,3072]{1,0:T(8,128)} %fusion.26), kind=kLoop, calls=%fused_computation | loop fusion | flops 19922944 | bytes 79691776 | tf_op jit(solution)/shard_map/concatenate | solution.py:191
  578.1 3.7 fusion.12
  581.8 3.8 fusion.13
  586.3 5.0 fusion.20
  591.3 38.6 %reduce-scatter.5.cloned.1.call-done = f32[176,1024]{1,0:T(8,128)} async-done(((f32[2816,1024]{1,0:T(8,128)}), f32[176,1024]{1,0:T(8,128)}) %reduce-scatter.5.cloned.1.call-update) | async-done | bytes 720912 | tf_op jit(solution)/shard_map/reduce_scatter | solution.py:196
  629.9 1.9 convert_element_type.173
  631.8 385.7 %reduce-scatter.3.cloned.1.call-done = f32[64,9728]{1,0:T(8,128)} async-done(((f32[1024,9728]{1,0:T(8,128)}), f32[64,9728]{1,0:T(8,128)}) %reduce-scatter.3.cloned.1.call-update) | async-done | bytes 2490384 | tf_op jit(solution)/shard_map/reduce_scatter | solution.py:190
  1017.5 1.8 convert.61
  1020.8 0.9 slice.173
  1021.8 5.0 fusion.138
  1028.0 45.8 %all-reduce.3.cloned.1.call-done = (bf16[64,3072]{1,0:T(8,128)(2,1)}, bf16[64,1024]{1,0:T(8,128)(2,1)}, bf16[64,5632]{1,0:T(8,128)(2,1)}, bf16[176,1024]{1,0:T(8,128)(2,1)}) async-done(((bf16[64,3072]{1,0:T(8,128)(2,1)}, bf16[64,1024]{1,0:T(8,128)(2,1)}, bf16[64,5632]{1,0:T(8,128)(2,1)}, bf16[176,1024]{1,0:T(8,128)(2,1)}), (bf16[64,3072]{1,0:T(8,128)(2,1)}, bf16[64,1024]{1,0:T(8,128)(2,1)}, ...) | async-done | bytes 1605648 | tf_op jit(solution)/shard_map/psum | solution.py:200
  1073.8 1.7 convert_element_type.171
  1075.5 1.9 convert_element_type.170
  1077.4 1.9 convert_element_type.174
  1079.3 1.2 convert_element_type.172
  (234 shorter events, 19.6 us)
Async XLA Ops:
  7.2 447.7 %all-gather.4.cloned.1.call-start = ((), (), s32[]{:S(2)}) async-start(), calls=%async_computation.2 | async-start | bytes 6684672 | tf_op jit(solution)/shard_map/all_gather | solution.py:108
  7.9 460.6 %all-gather.6.cloned.1.call-start = ((), (), s32[]{:S(2)}) async-start(), calls=%async_computation.3 | async-start | bytes 2228224 | tf_op jit(solution)/shard_map/all_gather | solution.py:109
  7.9 2.5 collective-permute-start
  12.3 44.3 %collective-permute-start.1 = (bf16[128,5632]{1,0:T(8,128)(2,1)S(1)}, bf16[128,5632]{1,0:T(8,128)(2,1)}, u32[]{:S(2)}, u32[]{:S(2)}) collective-permute-start(bf16[128,5632]{1,0:T(8,128)(2,1)S(1)} %maximum_select_fusion.3), channel_id=1, source_target_pairs={{0,2},{1,3},{2,0},{3,1},{4,6},{5,7},{6,4},{7,5},{8,10},{9,11},{10,... | collective-permute-start | bytes 4325384 | tf_op jit(solution)/shard_map/ppermute | solution.py:14
  59.6 88.1 %collective-permute-start.2 = (bf16[256,5632]{1,0:T(8,128)(2,1)S(1)}, bf16[256,5632]{1,0:T(8,128)(2,1)}, u32[]{:S(2)}, u32[]{:S(2)}) collective-permute-start(bf16[256,5632]{1,0:T(8,128)(2,1)S(1)} %maximum_select_fusion.2), channel_id=1, source_target_pairs={{0,4},{1,5},{2,6},{3,7},{4,0},{5,1},{6,2},{7,3},{8,12},{9,13},{10,... | collective-permute-start | bytes 8650760 | tf_op jit(solution)/shard_map/ppermute | solution.py:14
  61.2 424.4 %all-gather.8.cloned.1.call-start = ((), (), s32[]{:S(2)}) async-start(), calls=%async_computation.4 | async-start | bytes 6127616 | tf_op jit(solution)/shard_map/all_gather | solution.py:111
  61.2 96.0 %copy-start.69 = (s32[2,1]{0,1:T(1,128)S(1)}, s32[2,1]{0,1:T(1,128)}, u32[]{:S(2)}) copy-start(s32[2,1]{0,1:T(1,128)} %param.8) | copy-start | bytes 28
  61.2 98.6 %copy-start.5 = (bf16[2,1,64,1024]{3,2,1,0:T(8,128)(2,1)S(1)}, bf16[2,1,64,1024]{3,2,1,0:T(8,128)(2,1)}, u32[]{:S(2)}) copy-start(bf16[2,1,64,1024]{3,2,1,0:T(8,128)(2,1)} %param.7) | copy-start | bytes 786436
  61.3 99.2 %copy-start.41 = (bf16[2,1,64,1024]{3,2,1,0:T(8,128)(2,1)S(1)}, bf16[2,1,64,1024]{3,2,1,0:T(8,128)(2,1)}, u32[]{:S(2)}) copy-start(bf16[2,1,64,1024]{3,2,1,0:T(8,128)(2,1)} %param.13) | copy-start | bytes 786436
  154.6 283.6 %collective-permute-start.3 = (bf16[512,5632]{1,0:T(8,128)(2,1)}, bf16[512,5632]{1,0:T(8,128)(2,1)}, u32[]{:S(2)}, u32[]{:S(2)}) collective-permute-start(bf16[512,5632]{1,0:T(8,128)(2,1)} %maximum_select_fusion.1), channel_id=1, source_target_pairs={{0,8},{1,9},{2,10},{3,11},{4,12},{5,13},{6,14},{7,15},{8,0},{9,1},... | collective-permute-start | bytes 17301512 | tf_op jit(solution)/shard_map/ppermute | solution.py:14
  157.1 472.8 %reduce-scatter.5.cloned.1.call-start = ((), (), s32[]{:S(2)}) async-start(), calls=%async_computation.6 | async-start | bytes 12255232 | tf_op jit(solution)/shard_map/reduce_scatter | solution.py:196
  160.0 294.8 %copy-start.53 = (f32[64]{0:T(128)}, f32[64]{0:T(128)S(1)}, u32[]{:S(2)}) copy-start(f32[64]{0:T(128)S(1)} %get-tuple-element.100) | copy-start | bytes 772
  160.0 294.8 %copy-start.55 = (f32[64]{0:T(128)}, f32[64]{0:T(128)S(1)}, u32[]{:S(2)}) copy-start(f32[64]{0:T(128)S(1)} %get-tuple-element.101) | copy-start | bytes 772
  160.3 294.5 %copy-start.61 = (f32[64]{0:T(128)}, f32[64]{0:T(128)S(1)}, u32[]{:S(2)}) copy-start(f32[64]{0:T(128)S(1)} %add_rsqrt_fusion.3) | copy-start | bytes 772
  160.3 294.5 %copy-start.63 = (f32[64]{0:T(128)}, f32[64]{0:T(128)S(1)}, u32[]{:S(2)}) copy-start(f32[64]{0:T(128)S(1)} %add_rsqrt_fusion.1) | copy-start | bytes 772
  161.4 293.4 %copy-start.29 = (bf16[64,1024]{1,0:T(8,128)(2,1)}, bf16[64,1024]{1,0:T(8,128)(2,1)S(1)}, u32[]{:S(2)}) copy-start(bf16[64,1024]{1,0:T(8,128)(2,1)S(1)} %get-tuple-element.64) | copy-start | bytes 393220
  161.4 298.1 %copy-start.31 = (bf16[64,1024]{1,0:T(8,128)(2,1)}, bf16[64,1024]{1,0:T(8,128)(2,1)S(1)}, u32[]{:S(2)}) copy-start(bf16[64,1024]{1,0:T(8,128)(2,1)S(1)} %get-tuple-element.65) | copy-start | bytes 393220
  459.1 8.4 copy-start.35
  466.4 4.6 copy-start.10
  467.5 5.0 copy-start.49
  468.5 4.4 copy-start
  468.5 4.5 copy-start.6
  473.0 9.2 slice-start
  474.6 7.7 copy-start.16
  474.6 7.7 slice-start.1
  474.6 7.7 slice-start.2
  485.6 5.9 copy-start.1
  485.6 6.0 copy-start.18
  485.6 6.0 copy-start.42
  501.5 516.0 %reduce-scatter.3.cloned.1.call-start = ((), (), s32[]{:S(2)}) async-start(), calls=%async_computation.5 | async-start | bytes 42336256 | tf_op jit(solution)/shard_map/reduce_scatter | solution.py:190
  501.5 8.3 copy-start.25
  501.6 8.3 copy-start.27
  501.6 8.3 copy-start.58
  501.6 8.3 copy-start.66
  509.9 9.6 copy-start.3
  509.9 9.6 copy-start.43
  509.9 9.6 copy-start.60
  509.9 9.6 copy-start.68
  533.9 7.1 copy-start.17
  533.9 7.1 copy-start.23
  533.9 7.1 copy-start.24
  533.9 7.1 copy-start.26
  533.9 7.1 copy-start.28
  577.0 4.8 copy-start.22
  577.0 496.7 %all-reduce.3.cloned.1.call-start = ((), (), s32[]{:S(2)}) async-start(), calls=%async_computation.7 | async-start | bytes 3211264 | tf_op jit(solution)/shard_map/psum | solution.py:200
  1021.8 5.1 copy-start.39
  1021.8 5.1 copy-start.40
  1073.8 5.5 copy-start.44
  (35 other events, 64.4 us)
Sparse Core Ops, SparseCore 0:
  10.3 76.1 all-gather.3
  88.6 50.2 all-gather.5
  157.2 187.3 all-gather.7
  501.6 128.2 reduce-scatter.4
  634.6 382.7 reduce-scatter.2
  1021.8 51.8 all-reduce.2
